TPU v7x, 32 devices: a whole 2x2x4 slice. The times are simulated.
32 devices in a mesh: row: 4 (over z), col: 8 (over y, x, core).
Axes of the slice: x: 2, y: 2, z: 4, core: 2. Of those that a mesh axis runs over, the one named last changes fastest.
Arguments:
- trailing: float32 [16384, 16384], P('row', 'col'), may hold values from -51 to 51
- panel_cols: float32 [16384, 128], P(('row', 'col')), as said below
Outputs:
- updated: float32 [16384, 16384], P('row', 'col')
- triangle: float32 [128, 128], replicated
Inputs may be any that keep to these rules, and one draw needn't show every extreme that they name: panel_cols has full column rank.
All inputs are finite; a program needn't handle non-finite values.
Results may differ from a plain program's by a relative error of at most 0.00005.
Values sent between devices are 32-bit elements; how exact they have to be, the bound alone decides.
No kernel may reach another device: no remote copies, remote signals or barrier semaphores. Data moves between devices by JAX's collectives and lax.ppermute only.
A program may use at most 128 MiB of HBM per device.

v0:
```python
import jax
import jax.numpy as jnp
from jax import lax
from jax.sharding import PartitionSpec as P


def spread(array, axis, root):
    mine = lax.axis_index(axis) == root
    return lax.psum(jnp.where(mine, array, jnp.zeros_like(array)), axis)


def matmul(left_side, right_side):
    return jnp.dot(
        left_side, right_side, precision=lax.Precision.HIGHEST, preferred_element_type=jnp.float32
    )


def local(trailing, panel_cols):
    rows_here = trailing.shape[0]
    cols_here = trailing.shape[1]
    blocks_per = rows_here // cols_here
    row_index = lax.axis_index("row")
    col_index = lax.axis_index("col")
    gram_sum = lax.psum(matmul(panel_cols.T, panel_cols), ("row", "col"))
    factor = jnp.linalg.cholesky(gram_sum)
    basis_own = lax.linalg.triangular_solve(factor, panel_cols.T, left_side=True, lower=True).T
    basis_all = lax.all_gather(basis_own, ("row", "col"), axis=0, tiled=True)
    basis_rows = lax.dynamic_slice_in_dim(basis_all, row_index * rows_here, rows_here, 0)
    basis_cols = lax.dynamic_slice_in_dim(basis_all, col_index * cols_here, cols_here, 0)
    partial_value = matmul(trailing, basis_cols)
    image_rows = lax.psum(partial_value, "col")
    coupling = lax.psum(matmul(basis_rows.T, image_rows), "row")
    shift_rows = 2.0 * image_rows - 2.0 * matmul(basis_rows, coupling)
    shift_part = lax.dynamic_slice_in_dim(
        shift_rows, col_index % blocks_per * cols_here, cols_here, 0
    )
    shift_cols = spread(shift_part, "row", col_index // blocks_per)
    left_side = jnp.concatenate([basis_rows, shift_rows], axis=1)
    right_side = jnp.concatenate([shift_cols, basis_cols], axis=1)
    updated = trailing - matmul(left_side, right_side.T)
    return (updated, factor.T)


def solution(mesh):
    in_specs = (P("row", "col"), P(("row", "col"), None))
    out_specs = (P("row", "col"), P())
    return jax.shard_map(local, mesh=mesh, in_specs=in_specs, out_specs=out_specs, check_vma=False)
```

profile of v0, /device:TPU:0, one launch (start us, length us, event | category | flops | bytes accessed | tf_op | source)
XLA Modules:
  0.0 478.7 jit_solution(13148637477328393549)
XLA Ops:
  7.2 0.9 copy-done
  8.1 1.2 fusion.11
  9.4 126.9 %all-reduce.5.cloned.1.call-done = f32[128,128]{0,1:T(8,128)} async-done(((f32[128,128]{0,1:T(8,128)}), f32[128,128]{0,1:T(8,128)}) %all-reduce.5.cloned.1.call-update) | async-done | bytes 65552 | tf_op jit(solution)/shard_map/psum | solution.py:24
  136.3 0.9 copy.5
  137.2 0.9 fusion.8
  138.1 11.7 %cholesky.16 = f32[128,128]{1,0:T(8,128)S(1)} custom-call(f32[128,128]{1,0:T(8,128)S(1)} %fusion.8), custom_call_target="Cholesky" | custom-call | tf_op jit(solution)/shard_map/jit(cholesky)/cholesky | solution.py:25
  149.8 0.6 compare_reduce_fusion
  150.5 0.7 fusion.9
  151.1 9.8 %custom-call.6 = f32[1,128,128]{1,2,0:T(8,128)S(1)} custom-call(f32[1,128,128]{2,1,0:T(8,128)S(1)} %get-tuple-element.5), custom_call_target="InvertDiagBlocksLowerTriangular" | custom-call | tf_op jit(solution)/shard_map/triangular_solve | solution.py:26
  160.9 1.1 convolution_bitcast_fusion.1
  162.3 78.6 %all-gather.2.cloned.1.call-done = f32[16384,128]{0,1:T(8,128)} async-done(((f32[512,128]{0,1:T(8,128)}), f32[16384,128]{0,1:T(8,128)}) %all-gather.2.cloned.1.call-update) | async-done | bytes 8388624 | tf_op jit(solution)/shard_map/all_gather | solution.py:27
  240.9 1.3 constant_dynamic-slice_fusion
  242.2 38.6 %convolution_bitcast_fusion = f32[4096,128]{0,1:T(8,128)} fusion(f32[2048,128]{0,1:T(8,128)S(1)} %constant_dynamic-slice_fusion, f32[4096,2048]{1,0:T(8,128)} %param.2), kind=kOutput, calls=%fused_computation.3 | convolution fusion | flops 12884901888 | bytes 36700160 | tf_op jit(solution)/shard_map/dot_general | solution.py:13
  280.9 1.7 constant_dynamic-slice_fusion.1
  282.7 59.4 %all-reduce.7.cloned.1.call-done = f32[4096,128]{0,1:T(8,128)} async-done(((f32[4096,128]{0,1:T(8,128)}), f32[4096,128]{0,1:T(8,128)}) %all-reduce.7.cloned.1.call-update) | async-done | bytes 2097168 | tf_op jit(solution)/shard_map/psum | solution.py:31
  342.0 4.1 fusion.12
  346.1 0.3 all-reduce.11.cloned.1.call-start
  346.4 33.2 %all-reduce.9.cloned.1.call-done = f32[128,128]{1,0:T(8,128)} async-done(((f32[128,128]{1,0:T(8,128)}), f32[128,128]{1,0:T(8,128)}) %all-reduce.9.cloned.1.call-update) | async-done | bytes 65552 | tf_op jit(solution)/shard_map/psum | solution.py:32
  379.6 3.8 fusion
  383.4 1.3 copy-done.2
  384.8 1.0 dynamic-slice_select_fusion
  385.8 0.7 copy.6
  386.6 51.0 %all-reduce.11.cloned.1.call-done = f32[2048,128]{0,1:T(8,128)} async-done(((f32[2048,128]{0,1:T(8,128)}), f32[2048,128]{0,1:T(8,128)}) %all-reduce.11.cloned.1.call-update) | async-done | bytes 1048592 | tf_op jit(solution)/shard_map/psum | solution.py:9
  437.6 34.6 %convolution_subtract_fusion = f32[4096,2048]{1,0:T(8,128)} fusion(f32[4096,2048]{1,0:T(8,128)} %param.2, f32[4096,128]{0,1:T(8,128)} %copy-done.2, f32[4096,128]{0,1:T(8,128)S(1)} %constant_dynamic-slice_fusion.1, f32[2048,128]{0,1:T(8,128)S(1)} %constant_dynamic-slice_fusion, f32[2048,128]{0,1:T(8,128)} %all-reduce.11.cloned.1.call-done), kind=kOutput, calls=%fused_computation | convolution fusion | flops 25779765248 | bytes 73400320 | tf_op jit(solution)/shard_map/dot_general | solution.py:13
  (14 shorter events, 0.5 us)
Async XLA Ops:
  7.2 1.0 copy-start
  7.2 129.1 %all-reduce.5.cloned.1.call-start = ((), (), s32[]{:S(2)}) async-start(), calls=%async_computation | async-start | bytes 131072 | tf_op jit(solution)/shard_map/psum | solution.py:24
  9.4 231.6 %all-gather.2.cloned.1.call-start = ((), (), s32[]{:S(2)}) async-start(), calls=%async_computation.1 | async-start | bytes 8650752 | tf_op jit(solution)/shard_map/all_gather | solution.py:27
  162.1 179.9 %all-reduce.7.cloned.1.call-start = ((), (), s32[]{:S(2)}) async-start(), calls=%async_computation.2 | async-start | bytes 4194304 | tf_op jit(solution)/shard_map/psum | solution.py:31
  280.8 98.8 %all-reduce.9.cloned.1.call-start = ((), (), s32[]{:S(2)}) async-start(), calls=%async_computation.3 | async-start | bytes 131072 | tf_op jit(solution)/shard_map/psum | solution.py:32
  346.1 91.5 %all-reduce.11.cloned.1.call-start = ((), (), s32[]{:S(2)}) async-start(), calls=%async_computation.4 | async-start | bytes 2097152 | tf_op jit(solution)/shard_map/psum | solution.py:9
  383.4 1.3 copy-start.2
  437.6 34.6 %copy-start.1 = (f32[512,128]{1,0:T(8,128)S(1)}, f32[512,128]{1,0:T(8,128)}, u32[]{:S(2)}) copy-start(f32[512,128]{1,0:T(8,128)} %param.3) | copy-start | bytes 786436
Sparse Core Ops, SparseCore 0:
  14.1 122.0 all-reduce.4
  162.2 78.6 all-gather.1
  281.0 60.9 all-reduce.6
  346.2 33.3 all-reduce.8
  386.0 51.5 all-reduce.10
where the time goes:
time: 479 us
  waiting for transfers between devices  349 us (73%)
  matrix products  83.4 us (17%)
  other arithmetic  24.8 us (5%)
  between operations  13.9 us (3%)
  local copies, waits for them, and re-layouts  6.96 us (1%)
    psum x1, waiting for transfers between devices, local(): gram_sum = lax.psum(matmul(panel_cols.T, panel_cols), ('row', 'col'))  127 us
    dot_general x5, matrix products, matmul(): jnp.dot(left_side, right_side, precision=lax.Precision.HIGHEST, preferred...  82.2 us
    all_gather x1, waiting for transfers between devices, local(): basis_all = lax.all_gather(basis_own, ('row', 'col'), axis=0, tiled=True)  78.6 us
    psum x1, waiting for transfers between devices, local(): image_rows = lax.psum(partial_value, 'col')  59.4 us
    psum x1, waiting for transfers between devices, spread(): return lax.psum(jnp.where(mine, array, jnp.zeros_like(array)), axis)  51 us
    psum x1, waiting for transfers between devices, local(): coupling = lax.psum(matmul(basis_rows.T, image_rows), 'row')  33.2 us
    another operation x3, other arithmetic, local(): factor = jnp.linalg.cholesky(gram_sum)  12.4 us
    another operation x1, other arithmetic, local(): lax.linalg.triangular_solve(factor, panel_cols.T, left_side=True, lower=T...  9.81 us
  transfers between devices with their start and end apart: 5, of which 5 were waited for; matrix products, arithmetic and copies ran while one was open for 1% of the time, Pallas kernels for 0%

commit v1 on v0

--- a/solution.py
+++ b/solution.py
@@ -28,7 +28,11 @@
     basis_rows = lax.dynamic_slice_in_dim(basis_all, row_index * rows_here, rows_here, 0)
     basis_cols = lax.dynamic_slice_in_dim(basis_all, col_index * cols_here, cols_here, 0)
     partial_value = matmul(trailing, basis_cols)
-    image_rows = lax.psum(partial_value, "col")
+    image_rows = partial_value
+    for hop in (1, 2, 4):
+        image_rows = image_rows + lax.ppermute(
+            image_rows, "col", [(dev, dev ^ hop) for dev in range(8)]
+        )
     coupling = lax.psum(matmul(basis_rows.T, image_rows), "row")
     shift_rows = 2.0 * image_rows - 2.0 * matmul(basis_rows, coupling)
     shift_part = lax.dynamic_slice_in_dim(

time: 479 us -> 520 us (1.086)
  waiting for transfers between devices: 349 us -> 384 us
    ppermute x0 -> x3, waiting for transfers between devices: none -> 94.3 us  [local(): lax.ppermute(image_rows, 'col', [(dev, dev ^ hop) for dev in range(8)])]
    psum x1 -> x0, waiting for transfers between devices: 59.4 us -> none  [local(): image_rows = lax.psum(partial_value, 'col')]
  transfers between devices with their start and end apart: 5 -> 7, of which waited for: 5 -> 7; matrix products, arithmetic and copies ran while one was open for 1% -> 0% of each run, Pallas kernels for 0% -> 0%
where the time goes in v1:
time: 520 us
  waiting for transfers between devices  384 us (74%)
  matrix products  84.3 us (16%)
  other arithmetic  26.6 us (5%)
  between operations  13.9 us (3%)
  local copies, waits for them, and re-layouts  6.94 us (1%)
    psum x1, waiting for transfers between devices, local(): gram_sum = lax.psum(matmul(panel_cols.T, panel_cols), ('row', 'col'))  127 us
    ppermute x3, waiting for transfers between devices, local(): lax.ppermute(image_rows, 'col', [(dev, dev ^ hop) for dev in range(8)])  94.3 us
    dot_general x5, matrix products, matmul(): jnp.dot(left_side, right_side, precision=lax.Precision.HIGHEST, preferred...  83.2 us
    all_gather x1, waiting for transfers between devices, local(): basis_all = lax.all_gather(basis_own, ('row', 'col'), axis=0, tiled=True)  78.6 us
    psum x1, waiting for transfers between devices, spread(): return lax.psum(jnp.where(mine, array, jnp.zeros_like(array)), axis)  51 us
    psum x1, waiting for transfers between devices, local(): coupling = lax.psum(matmul(basis_rows.T, image_rows), 'row')  33.4 us
    another operation x3, other arithmetic, local(): factor = jnp.linalg.cholesky(gram_sum)  12.4 us
  transfers between devices with their start and end apart: 7, of which 7 were waited for; matrix products, arithmetic and copies ran while one was open for 0% of the time, Pallas kernels for 0%

profile of v1, /device:TPU:0, one launch (start us, length us, event | category | flops | bytes accessed | tf_op | source)
XLA Modules:
  0.0 519.8 jit_solution(5869287542383825536)
XLA Ops:
  7.2 0.9 copy-done
  8.1 1.2 fusion.12
  9.4 126.9 %all-reduce.4.cloned.1.call-done = f32[128,128]{0,1:T(8,128)} async-done(((f32[128,128]{0,1:T(8,128)}), f32[128,128]{0,1:T(8,128)}) %all-reduce.4.cloned.1.call-update) | async-done | bytes 65552 | tf_op jit(solution)/shard_map/psum | solution.py:24
  136.3 0.9 copy.5
  138.1 11.7 %cholesky.16 = f32[128,128]{1,0:T(8,128)S(1)} custom-call(f32[128,128]{1,0:T(8,128)S(1)} %fusion.9), custom_call_target="Cholesky" | custom-call | tf_op jit(solution)/shard_map/jit(cholesky)/cholesky | solution.py:25
  151.1 9.8 %custom-call.6 = f32[1,128,128]{1,2,0:T(8,128)S(1)} custom-call(f32[1,128,128]{2,1,0:T(8,128)S(1)} %get-tuple-element.5), custom_call_target="InvertDiagBlocksLowerTriangular" | custom-call | tf_op jit(solution)/shard_map/triangular_solve | solution.py:26
  160.9 1.1 convolution_bitcast_fusion.1
  162.3 78.6 %all-gather.2.cloned.1.call-done = f32[16384,128]{0,1:T(8,128)} async-done(((f32[512,128]{0,1:T(8,128)}), f32[16384,128]{0,1:T(8,128)}) %all-gather.2.cloned.1.call-update) | async-done | bytes 8388624 | tf_op jit(solution)/shard_map/all_gather | solution.py:27
  240.9 1.3 constant_dynamic-slice_fusion
  242.2 38.2 %convolution_bitcast_fusion = f32[4096,128]{0,1:T(8,128)S(1)} fusion(f32[2048,128]{0,1:T(8,128)S(1)} %constant_dynamic-slice_fusion, f32[4096,2048]{1,0:T(8,128)} %param.2), kind=kOutput, calls=%fused_computation.2 | convolution fusion | flops 12884901888 | bytes 36700160 | tf_op jit(solution)/shard_map/dot_general | solution.py:13
  280.7 3.9 collective-permute-done
  284.9 1.5 collective-permute-start.1
  286.4 46.3 %collective-permute-done.1 = f32[4096,128]{0,1:T(8,128)S(1)} collective-permute-done((f32[4096,128]{0,1:T(8,128)S(1)}, f32[4096,128]{0,1:T(8,128)S(1)}, u32[]{:S(2)}, u32[]{:S(2)}) %collective-permute-start.1) | collective-permute-done | bytes 2097184 | tf_op jit(solution)/shard_map/ppermute | solution.py:33
  332.8 1.5 add.44
  334.3 1.5 collective-permute-start.2
  335.8 1.7 constant_dynamic-slice_fusion.1
  337.5 44.0 %collective-permute-done.2 = f32[4096,128]{0,1:T(8,128)} collective-permute-done((f32[4096,128]{0,1:T(8,128)}, f32[4096,128]{0,1:T(8,128)}, u32[]{:S(2)}, u32[]{:S(2)}) %collective-permute-start.2) | collective-permute-done | bytes 2097184 | tf_op jit(solution)/shard_map/ppermute | solution.py:33
  381.5 4.8 fusion.6
  386.6 33.4 %all-reduce.6.cloned.1.call-done = f32[128,128]{1,0:T(8,128)} async-done(((f32[128,128]{1,0:T(8,128)}), f32[128,128]{1,0:T(8,128)}) %all-reduce.6.cloned.1.call-update) | async-done | bytes 65552 | tf_op jit(solution)/shard_map/psum | solution.py:36
  420.0 4.5 multiply_subtract_fusion
  424.5 1.3 copy-done.2
  425.9 1.1 dynamic-slice_select_fusion
  427.7 51.0 %all-reduce.8.cloned.1.call-done = f32[2048,128]{0,1:T(8,128)} async-done(((f32[2048,128]{0,1:T(8,128)}), f32[2048,128]{0,1:T(8,128)}) %all-reduce.8.cloned.1.call-update) | async-done | bytes 1048592 | tf_op jit(solution)/shard_map/psum | solution.py:9
  478.7 34.6 %convolution_subtract_fusion = f32[4096,2048]{1,0:T(8,128)} fusion(f32[4096,2048]{1,0:T(8,128)} %param.2, f32[4096,128]{0,1:T(8,128)} %copy-done.2, f32[4096,128]{0,1:T(8,128)S(1)} %constant_dynamic-slice_fusion.1, f32[2048,128]{0,1:T(8,128)S(1)} %constant_dynamic-slice_fusion, f32[2048,128]{0,1:T(8,128)} %all-reduce.8.cloned.1.call-done), kind=kOutput, calls=%fused_computation | convolution fusion | flops 25779765248 | bytes 73400320 | tf_op jit(solution)/shard_map/dot_general | solution.py:13
  (19 shorter events, 4.1 us)
Async XLA Ops:
  7.2 1.0 copy-start
  7.2 129.1 %all-reduce.4.cloned.1.call-start = ((), (), s32[]{:S(2)}) async-start(), calls=%async_computation | async-start | bytes 131072 | tf_op jit(solution)/shard_map/psum | solution.py:24
  9.4 231.6 %all-gather.2.cloned.1.call-start = ((), (), s32[]{:S(2)}) async-start(), calls=%async_computation.1 | async-start | bytes 8650752 | tf_op jit(solution)/shard_map/all_gather | solution.py:27
  162.1 257.9 %all-reduce.6.cloned.1.call-start = ((), (), s32[]{:S(2)}) async-start(), calls=%async_computation.2 | async-start | bytes 131072 | tf_op jit(solution)/shard_map/psum | solution.py:36
  280.4 4.2 collective-permute-start
  284.9 47.8 %collective-permute-start.1 = (f32[4096,128]{0,1:T(8,128)S(1)}, f32[4096,128]{0,1:T(8,128)S(1)}, u32[]{:S(2)}, u32[]{:S(2)}) collective-permute-start(f32[4096,128]{0,1:T(8,128)S(1)} %add.43), channel_id=1, source_target_pairs={{0,2},{1,3},{2,0},{3,1},{4,6},{5,7},{6,4},{7,5},{8,10},{9,11},{10,... | collective-permute-start | bytes 6291464 | tf_op jit(solution)/shard_map/ppermute | solution.py:33
  334.3 47.2 %collective-permute-start.2 = (f32[4096,128]{0,1:T(8,128)}, f32[4096,128]{0,1:T(8,128)}, u32[]{:S(2)}, u32[]{:S(2)}) collective-permute-start(f32[4096,128]{0,1:T(8,128)} %add.44), channel_id=1, source_target_pairs={{0,4},{1,5},{2,6},{3,7},{4,0},{5,1},{6,2},{7,3},{8,12},{9,13},{10,... | collective-permute-start | bytes 6291464 | tf_op jit(solution)/shard_map/ppermute | solution.py:33
  386.3 92.3 %all-reduce.8.cloned.1.call-start = ((), (), s32[]{:S(2)}) async-start(), calls=%async_computation.3 | async-start | bytes 2097152 | tf_op jit(solution)/shard_map/psum | solution.py:9
  424.5 1.3 copy-start.2
  478.7 34.6 %copy-start.1 = (f32[512,128]{1,0:T(8,128)S(1)}, f32[512,128]{1,0:T(8,128)}, u32[]{:S(2)}) copy-start(f32[512,128]{1,0:T(8,128)} %param.3) | copy-start | bytes 786436
Sparse Core Ops, SparseCore 0:
  14.1 122.0 all-reduce.3
  162.2 78.6 all-gather.1
  386.4 33.5 all-reduce.5
  427.1 51.5 all-reduce.7
